TPU v7x, 32 devices: a whole 2x2x4 slice. The times are simulated.
32 devices in a mesh: seq: 8 (over y, x, core), head: 4 (over z).
Axes of the slice: x: 2, y: 2, z: 4, core: 2. Of those that a mesh axis runs over, the one named last changes fastest.
Arguments:
- dna: bfloat16 [6144, 768], P('seq')
- conv_in: bfloat16 [5, 1536, 768], P(None, 'head')
- dilated_kernel_weight: bfloat16 [3, 1536, 1536], P(None, 'head'), may hold values from -0.09375 to 0.09375
- w_query: bfloat16 [1536, 1536], P('head')
- w_key: bfloat16 [1536, 1536], P('head')
- w_value: bfloat16 [1536, 1536], P('head'), may hold values from -0.15625 to 0.15625
- w_out: bfloat16 [1536, 1536], P('head'), may hold values from -0.21875 to 0.21875
Outputs:
- encoded: bfloat16 [3072, 1536], P('seq', 'head')
All inputs are finite; a program needn't handle non-finite values.
Results may differ from a plain program's by a relative error of at most 0.007.
Values may be sent and summed in bfloat16 or wider, within the bound.
No kernel may reach another device: no remote copies, remote signals or barrier semaphores. Data moves between devices by JAX's collectives and lax.ppermute only.
A program may use at most 64 MiB of HBM per device.

v0:
```python
import math
import jax
import jax.numpy as jnp
from jax import lax
from jax.sharding import PartitionSpec as P

C = 1536
HEAD_DIM = 64
KW = 5
DILATION_STEP = 4


def padded_2(block, sides, width):
    for axis, dim in sides:
        count = lax.axis_size(axis)
        forward = [(i, i + 1) for i in range(count - 1)]
        backward = [(target, source) for source, target in forward]
        low = lax.ppermute(
            lax.slice_in_dim(block, block.shape[dim] - width, None, axis=dim), axis, forward
        )
        high = lax.ppermute(lax.slice_in_dim(block, 0, width, axis=dim), axis, backward)
        block = jnp.concatenate([low, block, high], axis=dim)
    return block


def row_scale(hidden):
    squares = lax.psum(jnp.sum(hidden * hidden, axis=1), "head")
    return hidden * lax.rsqrt(squares / C + 1e-06)[:, None]


def reduce_operands(left, right):
    return lax.dot_general(
        left, right, (((1,), (1,)), ((), ())), preferred_element_type=jnp.float32
    )


def on_device(dna, conv_in, dilated_kernel_weight, w_query, w_key, w_value, w_out):
    local_row_count = dna.shape[0] // 2
    half = (KW - 1) // 2
    padded = padded_2(dna, (("seq", 0),), half)
    h1 = jnp.zeros((local_row_count, conv_in.shape[1]), jnp.float32)
    for kernel_offset in range(KW):
        rows = lax.slice(
            padded,
            (kernel_offset, 0),
            (kernel_offset + 2 * local_row_count - 1, padded.shape[1]),
            (2, 1),
        )
        h1 = h1 + reduce_operands(rows, conv_in[kernel_offset])
    gelu_output = jax.nn.gelu(row_scale(h1), approximate=True).astype(jnp.bfloat16)
    complete_output = lax.all_gather(gelu_output, "head", axis=1, tiled=True)
    broad_input = padded_2(complete_output, (("seq", 0),), DILATION_STEP)
    second_hidden = h1
    for kernel_offset in range(3):
        second_hidden = second_hidden + reduce_operands(
            broad_input[
                DILATION_STEP * kernel_offset : DILATION_STEP * kernel_offset + local_row_count
            ],
            dilated_kernel_weight[kernel_offset],
        )
    normed = row_scale(second_hidden).astype(jnp.bfloat16)
    local_width = w_query.shape[0]
    heads_here = local_width // HEAD_DIM
    empty = jnp.zeros((local_row_count, local_width), jnp.float32)
    totals = (empty, empty, empty)
    piece = lax.all_gather(normed, "head", axis=1, tiled=True)
    count = piece.shape[1]
    outs = []
    for total, weight in zip(totals, (w_query, w_key, w_value)):
        block = lax.slice_in_dim(weight, 0, count, axis=1)
        outs.append(total + reduce_operands(piece, block))
    q_acc, k_acc, v_acc = tuple(outs)
    query = q_acc.astype(jnp.bfloat16).reshape(local_row_count, heads_here, HEAD_DIM)
    keys = k_acc.astype(jnp.bfloat16)
    values = v_acc.astype(jnp.bfloat16)
    scale = 1.0 / math.sqrt(HEAD_DIM)
    start_state = (
        jnp.full((heads_here, local_row_count), -1e30, jnp.float32),
        jnp.zeros((heads_here, local_row_count), jnp.float32),
        jnp.zeros((local_row_count, heads_here, HEAD_DIM), jnp.float32),
    )
    key_rows = lax.all_gather(keys, "seq", axis=0, tiled=True)
    value_rows = lax.all_gather(values, "seq", axis=0, tiled=True)
    count = key_rows.shape[0]
    width = 512 if count % 512 == 0 else count
    blocks = count // width
    key_blocks = key_rows.reshape(blocks, width, heads_here, HEAD_DIM)
    value_blocks = value_rows.reshape(blocks, width, heads_here, HEAD_DIM)

    def step(state, operands):
        running, total, acc = state
        key_block, value_block = operands
        scores = (
            jnp.einsum("qhd,khd->hqk", query, key_block, preferred_element_type=jnp.float32) * scale
        )
        newest = jnp.maximum(running, jnp.max(scores, axis=2))
        factor = jnp.exp(running - newest)
        weights = jnp.exp(scores - newest[:, :, None])
        total = total * factor + jnp.sum(weights, axis=2)
        update = jnp.einsum(
            "hqk,khd->qhd",
            weights.astype(jnp.bfloat16),
            value_block,
            preferred_element_type=jnp.float32,
        )
        acc = acc * jnp.transpose(factor)[:, :, None] + update
        return ((newest, total, acc), None)

    state, _ = lax.scan(step, start_state, (key_blocks, value_blocks))
    running, total, acc = state
    attended = (
        (acc / jnp.transpose(total)[:, :, None])
        .reshape(local_row_count, local_width)
        .astype(jnp.bfloat16)
    )
    partial_out = jnp.dot(attended, w_out, preferred_element_type=jnp.float32)
    mixed = lax.psum_scatter(
        partial_out.astype(jnp.bfloat16), "head", scatter_dimension=1, tiled=True
    ).astype(jnp.float32)
    return (second_hidden + mixed).astype(jnp.bfloat16)


def solution(mesh):
    in_specs = (
        P("seq", None),
        P(None, "head", None),
        P(None, "head", None),
        P("head", None),
        P("head", None),
        P("head", None),
        P("head", None),
    )
    out_specs = P("seq", "head")
    return jax.shard_map(
        on_device, mesh=mesh, in_specs=in_specs, out_specs=out_specs, check_vma=False
    )
```

profile of v0, /device:TPU:0, one launch (start us, length us, event | category | flops | bytes accessed | tf_op | source)
XLA Modules:
  0.0 285.1 jit_solution(8050887976854538106)
XLA Ops:
  6.5 0.9 fusion.57
  7.4 2.3 collective-permute-start
  9.8 1.3 collective-permute-start.1
  11.1 5.0 %slice.65 = bf16[384,768]{1,0:T(8,128)(2,1)S(1)} slice(bf16[768,768]{1,0:T(8,128)(2,1)} %param.9), slice={[0:767:2], [0:768:1]} | slice | bytes 1179648 | tf_op jit(solution)/shard_map/slice | solution.py:43
  16.1 2.4 fusion.44
  18.5 3.5 %slice.67 = bf16[384,768]{1,0:T(8,128)(2,1)} slice(bf16[768,768]{1,0:T(8,128)(2,1)S(1)} %copy-done.1), slice={[1:768:2], [0:768:1]} | slice | bytes 1179648 | tf_op jit(solution)/shard_map/slice | solution.py:43
  22.1 1.0 pad_maximum_fusion
  23.0 3.7 %slice.69 = bf16[384,768]{1,0:T(8,128)(2,1)} slice(bf16[772,768]{1,0:T(8,128)(2,1)S(1)} %pad_maximum_fusion), slice={[4:771:2], [0:768:1]} | slice | bytes 1179648 | tf_op jit(solution)/shard_map/slice | solution.py:43
  26.7 1.1 slice.63
  27.8 3.6 %slice.61 = bf16[384,768]{1,0:T(8,128)(2,1)} slice(bf16[772,768]{1,0:T(8,128)(2,1)S(1)} %pad_maximum_fusion), slice={[0:767:2], [0:768:1]} | slice | bytes 1179648 | tf_op jit(solution)/shard_map/slice | solution.py:43
  31.4 1.6 fusion.46
  33.0 1.8 fusion.24
  34.9 1.6 convolution_add_fusion.1
  36.4 1.6 multiply_reduce_fusion.1
  38.0 12.8 %psum.14 = f32[384]{0:T(512)S(1)} all-reduce(f32[384]{0:T(512)S(1)} %get-tuple-element.105), channel_id=1, replica_groups=mesh['seq'=8,'head'=4] {'head'}, use_global_device_ids=true, to_apply=%region_1.0 | all-reduce | flops 384 | bytes 3072 | tf_op jit(solution)/shard_map/psum | solution.py:27
  50.8 0.9 fusion.41
  51.8 0.0 all-gather.5.cloned.1.call-update
  51.8 0.0 all-gather.7.cloned.1.call-start
  51.8 31.3 %all-gather.5.cloned.1.call-done = bf16[384,1536]{0,1:T(8,128)(2,1)} async-done(((bf16[384,384]{0,1:T(8,128)(2,1)}), bf16[384,1536]{0,1:T(8,128)(2,1)}) %all-gather.5.cloned.1.call-update) | async-done | bytes 1179664 | tf_op jit(solution)/shard_map/all_gather | solution.py:51
  83.1 1.4 fusion.56
  84.6 1.4 collective-permute-start.3
  86.0 3.1 %collective-permute-start.2 = (bf16[4,1536]{0,1:T(8,128)(2,1)S(1)}, bf16[4,1536]{0,1:T(8,128)(2,1)S(1)}, u32[]{:S(2)}, u32[]{:S(2)}) collective-permute-start(bf16[4,1536]{0,1:T(8,128)(2,1)S(1)} %get-tuple-element.102), channel_id=1, source_target_pairs={{0,4},{4,8},{8,12},{12,16},{16,20},{20,24},{24,28},{1,5},{5,9},{9,... | collective-permute-start | bytes 36872 | tf_op jit(solution)/shard_map/ppermute | solution.py:18
  89.1 2.4 fusion.28
  91.5 0.9 fusion.23
  92.4 0.9 multiply_reduce_fusion
  93.3 9.9 %psum.15 = f32[384]{0:T(512)S(1)} all-reduce(f32[384]{0:T(512)S(1)} %get-tuple-element.107), channel_id=1, replica_groups=mesh['seq'=8,'head'=4] {'head'}, use_global_device_ids=true, to_apply=%region_3.0 | all-reduce | flops 384 | bytes 3072 | tf_op jit(solution)/shard_map/psum | solution.py:27
  103.2 0.8 multiply_convert_fusion
  104.0 0.0 all-gather.9.cloned.1.call-start
  104.1 35.4 %all-gather.7.cloned.1.call-done = bf16[384,1536]{0,1:T(8,128)(2,1)} async-done(((bf16[384,384]{0,1:T(8,128)(2,1)}), bf16[384,1536]{0,1:T(8,128)(2,1)}) %all-gather.7.cloned.1.call-update) | async-done | bytes 1179664 | tf_op jit(solution)/shard_map/all_gather | solution.py:66
  139.4 3.2 %convolution_convert_fusion.3 = bf16[384,384]{1,0:T(8,128)(2,1)} fusion(bf16[384,1536]{0,1:T(8,128)(2,1)} %all-gather.7.cloned.1.call-done, bf16[384,1536]{1,0:T(8,128)(2,1)} %param.13), kind=kOutput, calls=%fused_computation.34 | convolution fusion | flops 453132288 | bytes 2654208 | tf_op jit(solution)/shard_map/dot_general | solution.py:32
  142.6 0.0 all-gather.11.cloned.1.call-start
  142.7 3.2 %convolution_convert_fusion.2 = bf16[384,384]{1,0:T(8,128)(2,1)} fusion(bf16[384,1536]{0,1:T(8,128)(2,1)} %all-gather.7.cloned.1.call-done, bf16[384,1536]{1,0:T(8,128)(2,1)} %param.14), kind=kOutput, calls=%fused_computation.33 | convolution fusion | flops 453132288 | bytes 2654208 | tf_op jit(solution)/shard_map/dot_general | solution.py:32
  145.9 0.2 reduce-scatter.2.cloned.1.call-start
  146.1 2.4 convolution_convert_fusion.1
  148.5 22.4 %all-gather.9.cloned.1.call-done = bf16[3072,384]{1,0:T(8,128)(2,1)} async-done(((bf16[384,384]{1,0:T(8,128)(2,1)}), bf16[3072,384]{1,0:T(8,128)(2,1)}) %all-gather.9.cloned.1.call-update) | async-done | bytes 2359312 | tf_op jit(solution)/shard_map/all_gather | solution.py:82
  170.9 8.1 %reshape.19 = bf16[6,512,6,64]{3,2,1,0:T(8,128)(2,1)} reshape(bf16[3072,384]{1,0:T(8,128)(2,1)} %all-gather.9.cloned.1.call-done) | data formatting | bytes 4718592 | tf_op jit(solution)/shard_map/reshape | solution.py:87
  179.0 7.2 %copy.16 = bf16[6,512,6,64]{1,3,2,0:T(8,128)(2,1)} copy(bf16[6,512,6,64]{3,2,1,0:T(8,128)(2,1)} %reshape.19) | data formatting | bytes 4718592
  186.2 15.4 %all-gather.11.cloned.1.call-done = bf16[3072,384]{1,0:T(8,128)(2,1)} async-done(((bf16[384,384]{1,0:T(8,128)(2,1)}), bf16[3072,384]{1,0:T(8,128)(2,1)}) %all-gather.11.cloned.1.call-update) | async-done | bytes 2359312 | tf_op jit(solution)/shard_map/all_gather | solution.py:83
  201.7 8.1 %reshape.20 = bf16[6,512,6,64]{3,2,1,0:T(8,128)(2,1)} reshape(bf16[3072,384]{1,0:T(8,128)(2,1)} %all-gather.11.cloned.1.call-done) | data formatting | bytes 4718592 | tf_op jit(solution)/shard_map/reshape | solution.py:88
  209.8 7.1 %copy.17 = bf16[6,512,6,64]{1,3,2,0:T(8,128)(2,1)} copy(bf16[6,512,6,64]{3,2,1,0:T(8,128)(2,1)} %reshape.20) | data formatting | bytes 4718592
  216.9 28.4 %while.15 = (s32[]{:T(128)}, f32[6,384]{1,0:T(8,128)S(1)}, f32[6,384]{1,0:T(8,128)S(1)}, f32[384,6,64]{0,2,1:T(8,128)S(1)}, bf16[6,512,6,64]{1,3,2,0:T(8,128)(2,...) while((s32[]{:T(128)}, f32[6,384]{1,0:T(8,128)S(1)}, ...), condition=%wide.region_7.8_spmd.clone, body=%wide.region_4.7_spmd.clone.sunk | while | flops 311883264 | bytes 16564345 | solution.py:109
  216.9 1.8 bitcast_reduce_fusion.2
  218.8 0.8 fusion.84
  219.6 2.0 fusion.86
  221.7 1.8 bitcast_reduce_fusion.2
  223.5 0.8 fusion.84
  224.3 2.0 fusion.86
  226.4 1.8 bitcast_reduce_fusion.2
  228.2 0.8 fusion.84
  229.0 2.0 fusion.86
  231.1 1.8 bitcast_reduce_fusion.2
  233.0 0.8 fusion.84
  233.8 2.0 fusion.86
  235.8 1.8 bitcast_reduce_fusion.2
  237.7 0.8 fusion.84
  238.5 2.0 fusion.86
  240.6 1.8 bitcast_reduce_fusion.2
  242.4 0.8 fusion.84
  243.2 2.0 fusion.86
  245.3 0.1 divide_convert_fusion
  245.4 2.0 convolution_convert_fusion
  247.4 29.3 %reduce-scatter.2.cloned.1.call-done = bf16[384,384]{0,1:T(8,128)(2,1)} async-done(((bf16[384,1536]{0,1:T(8,128)(2,1)}), bf16[384,384]{0,1:T(8,128)(2,1)}) %reduce-scatter.2.cloned.1.call-update) | async-done | bytes 294928 | tf_op jit(solution)/shard_map/reduce_scatter | solution.py:117
  276.7 1.0 add_convert_fusion
  277.7 0.9 copy.19
  (46 shorter events, 0.3 us)
Async XLA Ops:
  6.5 238.8 %copy-start = (bf16[384,1536]{1,0:T(8,128)(2,1)S(1)}, bf16[384,1536]{1,0:T(8,128)(2,1)}, u32[]{:S(2)}) copy-start(bf16[384,1536]{1,0:T(8,128)(2,1)} %param.15) | copy-start | bytes 3538948
  6.5 12.0 %copy-start.1 = (bf16[768,768]{1,0:T(8,128)(2,1)S(1)}, bf16[768,768]{1,0:T(8,128)(2,1)}, u32[]{:S(2)}) copy-start(bf16[768,768]{1,0:T(8,128)(2,1)} %param.9) | copy-start | bytes 3538948
  6.5 76.6 %all-gather.5.cloned.1.call-start = ((), (), s32[]{:S(2)}) async-start(), calls=%async_computation.1 | async-start | bytes 1474560 | tf_op jit(solution)/shard_map/all_gather | solution.py:51
  7.4 14.6 %collective-permute-start = (bf16[2,768]{1,0:T(2,128)(2,1)S(1)}, bf16[2,768]{1,0:T(2,128)(2,1)S(1)}, u32[]{:S(2)}, u32[]{:S(2)}) collective-permute-start(bf16[2,768]{1,0:T(2,128)(2,1)S(1)} %get-tuple-element.103), channel_id=1, source_target_pairs={{0,4},{4,8},{8,12},{12,16},{16,20},{20,24},{24,28},{1,5},{5,9},{9,... | collective-permute-start | bytes 9224 | tf_op jit(solution)/shard_map/ppermute | solution.py:18
  9.8 12.3 %collective-permute-start.1 = (bf16[2,768]{1,0:T(2,128)(2,1)S(1)}, bf16[2,768]{1,0:T(2,128)(2,1)}, u32[]{:S(2)}, u32[]{:S(2)}) collective-permute-start(bf16[2,768]{1,0:T(2,128)(2,1)S(1)} %get-tuple-element.104), channel_id=1, source_target_pairs={{4,0},{8,4},{12,8},{16,12},{20,16},{24,20},{28,24},{5,1},{9,5},{13... | collective-permute-start | bytes 9224 | tf_op jit(solution)/shard_map/ppermute | solution.py:21
  26.7 6.3 %copy-start.2 = (f32[384,384]{0,1:T(8,128)S(1)}, f32[384,384]{0,1:T(8,128)}, u32[]{:S(2)}) copy-start(f32[384,384]{0,1:T(8,128)} %fusion.44) | copy-start | bytes 1769476
  31.4 3.5 %copy-start.3 = (bf16[384,768]{1,0:T(8,128)(2,1)S(1)}, bf16[384,768]{1,0:T(8,128)(2,1)}, u32[]{:S(2)}) copy-start(bf16[384,768]{1,0:T(8,128)(2,1)} %slice.67) | copy-start | bytes 1769476
  33.0 3.4 %copy-start.4 = (bf16[384,768]{1,0:T(8,128)(2,1)S(1)}, bf16[384,768]{1,0:T(8,128)(2,1)}, u32[]{:S(2)}) copy-start(bf16[384,768]{1,0:T(8,128)(2,1)} %slice.69) | copy-start | bytes 1769476
  51.8 87.7 %all-gather.7.cloned.1.call-start = ((), (), s32[]{:S(2)}) async-start(), calls=%async_computation.2 | async-start | bytes 1474560 | tf_op jit(solution)/shard_map/all_gather | solution.py:66
  83.1 8.4 %copy-start.5 = (bf16[384,1536]{0,1:T(8,128)(2,1)S(1)}, bf16[384,1536]{0,1:T(8,128)(2,1)}, u32[]{:S(2)}) copy-start(bf16[384,1536]{0,1:T(8,128)(2,1)} %all-gather.5.cloned.1.call-done) | copy-start | bytes 3538948
  83.1 8.4 %copy-start.6 = (bf16[3,384,1536]{2,1,0:T(8,128)(2,1)S(1)}, bf16[3,384,1536]{2,1,0:T(8,128)(2,1)}, u32[]{:S(2)}) copy-start(bf16[3,384,1536]{2,1,0:T(8,128)(2,1)} %param.11) | copy-start | bytes 10616836
  84.6 7.8 %collective-permute-start.3 = (bf16[4,1536]{0,1:T(8,128)(2,1)S(1)}, bf16[4,1536]{0,1:T(8,128)(2,1)S(1)}, u32[]{:S(2)}, u32[]{:S(2)}) collective-permute-start(bf16[4,1536]{0,1:T(8,128)(2,1)S(1)} %get-tuple-element.101), channel_id=1, source_target_pairs={{4,0},{8,4},{12,8},{16,12},{20,16},{24,20},{28,24},{5,1},{9,5},{13... | collective-permute-start | bytes 36872 | tf_op jit(solution)/shard_map/ppermute | solution.py:21
  86.0 5.5 %collective-permute-start.2 = (bf16[4,1536]{0,1:T(8,128)(2,1)S(1)}, bf16[4,1536]{0,1:T(8,128)(2,1)S(1)}, u32[]{:S(2)}, u32[]{:S(2)}) collective-permute-start(bf16[4,1536]{0,1:T(8,128)(2,1)S(1)} %get-tuple-element.102), channel_id=1, source_target_pairs={{0,4},{4,8},{8,12},{12,16},{16,20},{20,24},{24,28},{1,5},{5,9},{9,... | collective-permute-start | bytes 36872 | tf_op jit(solution)/shard_map/ppermute | solution.py:18
  104.0 66.9 %all-gather.9.cloned.1.call-start = ((), (), s32[]{:S(2)}) async-start(), calls=%async_computation.3 | async-start | bytes 2654208 | tf_op jit(solution)/shard_map/all_gather | solution.py:82
  142.6 59.1 %all-gather.11.cloned.1.call-start = ((), (), s32[]{:S(2)}) async-start(), calls=%async_computation.4 | async-start | bytes 2654208 | tf_op jit(solution)/shard_map/all_gather | solution.py:83
  145.9 130.8 %reduce-scatter.2.cloned.1.call-start = ((), (), s32[]{:S(2)}) async-start(), calls=%async_computation.5 | async-start | bytes 1474560 | tf_op jit(solution)/shard_map/reduce_scatter | solution.py:117
Sparse Core Ops, SparseCore 0:
  51.9 31.1 all-gather.4
  104.1 35.2 all-gather.6
  142.7 28.1 all-gather.8
  172.6 29.0 all-gather.10
  247.5 29.1 reduce-scatter.1
where the time goes:
time: 287 us; the launch traced here: 285 us
  waiting for transfers between devices  134 us (47%)
  local copies, waits for them, and re-layouts  50.8 us (18%)
  matrix products  47 us (16%)
  blocking collectives  22.7 us (8%)
  between operations  13.4 us (5%)
  other arithmetic  8.58 us (3%)
  starting transfers between devices  8.47 us (3%)
    all_gather x1, waiting for transfers between devices, on_device(): piece = lax.all_gather(normed, 'head', axis=1, tiled=True)  35.4 us
    all_gather x1, waiting for transfers between devices, on_device(): complete_output = lax.all_gather(gelu_output, 'head', axis=1, tiled=True)  31.3 us
    reduce_scatter x1, waiting for transfers between devices, on_device(): lax.psum_scatter(partial_out.astype(jnp.bfloat16), 'head', scatter_dimens...  29.3 us
    psum x2, blocking collectives, row_scale(): squares = lax.psum(jnp.sum(hidden * hidden, axis=1), 'head')  22.7 us
    all_gather x1, waiting for transfers between devices, on_device(): key_rows = lax.all_gather(keys, 'seq', axis=0, tiled=True)  22.4 us
    dot_general x11, matrix products, reduce_operands(): lax.dot_general(left, right, (((1,), (1,)), ((), ())), preferred_element_...  21.8 us
    slice x5, local copies, waits for them, and re-layouts, on_device(): lax.slice(padded, (kernel_offset, 0), (kernel_offset + 2 * local_row_coun...  17 us
    all_gather x1, waiting for transfers between devices, on_device(): value_rows = lax.all_gather(values, 'seq', axis=0, tiled=True)  15.4 us
  transfers between devices with their start and end apart: 9, of which 5 were waited for; matrix products, arithmetic and copies ran while one was open for 12% of the time, Pallas kernels for 0%

commit v1 on v0

--- a/solution.py
+++ b/solution.py
@@ -3,6 +3,7 @@
 import jax.numpy as jnp
 from jax import lax
 from jax.sharding import PartitionSpec as P
+from jax.lax import axis_index, axis_size, ppermute
 
 C = 1536
 HEAD_DIM = 64
@@ -79,7 +80,21 @@
         jnp.zeros((heads_here, local_row_count), jnp.float32),
         jnp.zeros((local_row_count, heads_here, HEAD_DIM), jnp.float32),
     )
-    key_rows = lax.all_gather(keys, "seq", axis=0, tiled=True)
+    n_dev_all = axis_size("seq")
+    steps_seen = []
+    for hop_no in range(n_dev_all):
+        steps_seen.append((hop_no, (hop_no + 1) % n_dev_all))
+    so_far_all = []
+    for hop_no in range(n_dev_all):
+        so_far_all.append((hop_no, (hop_no - 1) % n_dev_all))
+    current_arr, w2 = ([keys], [keys])
+    for _ in range(n_dev_all // 2):
+        tile_out = ppermute(current_arr[-1], "seq", steps_seen)
+        current_arr.append(tile_out)
+    for _ in range((n_dev_all - 1) // 2):
+        w2.append(ppermute(w2[-1], "seq", so_far_all))
+    carry_in = jnp.concatenate([*current_arr[::-1], *w2[1:]], axis=0)
+    key_rows = jnp.roll(carry_in, (axis_index("seq") - n_dev_all // 2) * keys.shape[0], axis=0)
     value_rows = lax.all_gather(values, "seq", axis=0, tiled=True)
     count = key_rows.shape[0]
     width = 512 if count % 512 == 0 else count

time: 287 us -> 320 us (1.11)
  matrix products: 47 us -> 68.6 us
  local copies, waits for them, and re-layouts: 50.8 us -> 63.2 us
  waiting for transfers between devices: 134 us -> 127 us
  starting transfers between devices: 8.47 us -> 14 us
    ppermute x0 -> x7, waiting for transfers between devices: none -> 31.3 us  [the longest x4 31.3 us: on_device(): tile_out = ppermute(current_arr[-1], 'seq', steps_seen)]
    all_gather x1 -> x0, waiting for transfers between devices: 22.4 us -> none  [on_device(): key_rows = lax.all_gather(keys, 'seq', axis=0, tiled=True)]
    all_gather x1, waiting for transfers between devices: 15.4 us -> 0.01 us  [on_device(): value_rows = lax.all_gather(values, 'seq', axis=0, tiled=True)]
    dot_general x6, matrix products: 11 us -> 23.7 us  [step(): jnp.einsum('qhd,khd->hqk', query, key_block, preferred_element_type=jnp.f...]
    dot_general x6, matrix products: 12.2 us -> 21.8 us  [step(): jnp.einsum('hqk,khd->qhd', weights.astype(jnp.bfloat16), value_block, pre...]
    unnamed x16 -> x35, local copies, waits for them, and re-layouts: 14.4 us -> 23.4 us
    ppermute x0 -> x7, starting transfers between devices: none -> 7.51 us  [the longest x3 7.44 us: on_device(): w2.append(ppermute(w2[-1], 'seq', so_far_all))]
  transfers between devices with their start and end apart: 9 -> 15, of which waited for: 5 -> 8; matrix products, arithmetic and copies ran while one was open for 12% -> 14% of each run, Pallas kernels for 0% -> 0%
where the time goes in v1:
time: 320 us; the launch traced here: 318 us
  waiting for transfers between devices  127 us (40%)
  matrix products  68.6 us (21%)
  local copies, waits for them, and re-layouts  63.2 us (20%)
  blocking collectives  22.7 us (7%)
  starting transfers between devices  14 us (4%)
  between operations  13.5 us (4%)
  other arithmetic  8.56 us (3%)
    all_gather x1, waiting for transfers between devices, on_device(): piece = lax.all_gather(normed, 'head', axis=1, tiled=True)  33.5 us
    ppermute x4, waiting for transfers between devices, on_device(): tile_out = ppermute(current_arr[-1], 'seq', steps_seen)  31.3 us
    all_gather x1, waiting for transfers between devices, on_device(): complete_output = lax.all_gather(gelu_output, 'head', axis=1, tiled=True)  31.3 us
    reduce_scatter x1, waiting for transfers between devices, on_device(): lax.psum_scatter(partial_out.astype(jnp.bfloat16), 'head', scatter_dimens...  30.1 us
    dot_general x6, matrix products, step(): jnp.einsum('qhd,khd->hqk', query, key_block, preferred_element_type=jnp.f...  23.7 us
    unnamed x35, local copies, waits for them, and re-layouts  23.4 us
    psum x2, blocking collectives, row_scale(): squares = lax.psum(jnp.sum(hidden * hidden, axis=1), 'head')  22.7 us
    dot_general x6, matrix products, step(): jnp.einsum('hqk,khd->qhd', weights.astype(jnp.bfloat16), value_block, pre...  21.8 us
  transfers between devices with their start and end apart: 15, of which 8 were waited for; matrix products, arithmetic and copies ran while one was open for 14% of the time, Pallas kernels for 0%

profile of v1, /device:TPU:0, one launch (start us, length us, event | category | flops | bytes accessed | tf_op | source)
XLA Modules:
  0.0 317.8 jit_solution(10461786832355247879)
XLA Ops:
  7.4 2.3 collective-permute-start
  9.8 1.3 collective-permute-start.1
  11.1 5.0 %slice.65 = bf16[384,768]{1,0:T(8,128)(2,1)S(1)} slice(bf16[768,768]{1,0:T(8,128)(2,1)} %param.9), slice={[0:767:2], [0:768:1]} | slice | bytes 1179648 | tf_op jit(solution)/shard_map/slice | solution.py:44
  16.1 2.4 fusion.44
  18.5 3.5 %slice.67 = bf16[384,768]{1,0:T(8,128)(2,1)} slice(bf16[768,768]{1,0:T(8,128)(2,1)S(1)} %copy-done.2), slice={[1:768:2], [0:768:1]} | slice | bytes 1179648 | tf_op jit(solution)/shard_map/slice | solution.py:44
  22.1 1.0 pad_maximum_fusion
  23.0 1.1 slice.63
  24.2 3.6 %slice.61 = bf16[384,768]{1,0:T(8,128)(2,1)} slice(bf16[772,768]{1,0:T(8,128)(2,1)S(1)} %pad_maximum_fusion), slice={[0:767:2], [0:768:1]} | slice | bytes 1179648 | tf_op jit(solution)/shard_map/slice | solution.py:44
  27.7 3.7 %slice.69 = bf16[384,768]{1,0:T(8,128)(2,1)} slice(bf16[772,768]{1,0:T(8,128)(2,1)S(1)} %pad_maximum_fusion), slice={[4:771:2], [0:768:1]} | slice | bytes 1179648 | tf_op jit(solution)/shard_map/slice | solution.py:44
  31.4 1.6 fusion.46
  33.1 1.8 fusion.24
  34.9 1.6 convolution_add_fusion.1
  36.5 1.6 multiply_reduce_fusion.1
  38.0 12.8 %psum.14 = f32[384]{0:T(512)S(1)} all-reduce(f32[384]{0:T(512)S(1)} %get-tuple-element.105), channel_id=1, replica_groups=mesh['seq'=8,'head'=4] {'head'}, use_global_device_ids=true, to_apply=%region_1.0 | all-reduce | flops 384 | bytes 3072 | tf_op jit(solution)/shard_map/psum | solution.py:28
  50.8 0.9 fusion.41
  51.8 31.3 %all-gather.4.cloned.1.call-done = bf16[384,1536]{0,1:T(8,128)(2,1)} async-done(((bf16[384,384]{0,1:T(8,128)(2,1)}), bf16[384,1536]{0,1:T(8,128)(2,1)}) %all-gather.4.cloned.1.call-update) | async-done | bytes 1179664 | tf_op jit(solution)/shard_map/all_gather | solution.py:52
  83.1 1.4 fusion.56
  84.6 1.4 collective-permute-start.2
  86.0 1.3 collective-permute-start.3
  87.3 2.4 fusion.28
  89.8 0.9 fusion.23
  91.3 0.9 multiply_reduce_fusion
  92.3 9.9 %psum.15 = f32[384]{0:T(512)S(1)} all-reduce(f32[384]{0:T(512)S(1)} %get-tuple-element.107), channel_id=1, replica_groups=mesh['seq'=8,'head'=4] {'head'}, use_global_device_ids=true, to_apply=%region_3.0 | all-reduce | flops 384 | bytes 3072 | tf_op jit(solution)/shard_map/psum | solution.py:28
  103.0 33.5 %all-gather.6.cloned.1.call-done = bf16[384,1536]{0,1:T(8,128)(2,1)} async-done(((bf16[384,384]{0,1:T(8,128)(2,1)}), bf16[384,1536]{0,1:T(8,128)(2,1)}) %all-gather.6.cloned.1.call-update) | async-done | bytes 1179664 | tf_op jit(solution)/shard_map/all_gather | solution.py:67
  136.4 3.2 convolution_convert_fusion.2
  139.7 2.4 convolution_convert_fusion.3
  142.2 7.0 %collective-permute-done.4 = bf16[384,384]{1,0:T(8,128)(2,1)S(1)} collective-permute-done((bf16[384,384]{1,0:T(8,128)(2,1)S(1)}, bf16[384,384]{1,0:T(8,128)(2,1)S(1)}, u32[]{:S(2)}, u32[]{:S(2)}) %collective-permute-start.4) | collective-permute-done | bytes 294944 | tf_op jit(solution)/shard_map/ppermute | solution.py:92
  149.2 2.6 collective-permute-start.8
  151.9 6.5 %collective-permute-done.5 = bf16[384,384]{1,0:T(8,128)(2,1)S(1)} collective-permute-done((bf16[384,384]{1,0:T(8,128)(2,1)S(1)}, bf16[384,384]{1,0:T(8,128)(2,1)S(1)}, u32[]{:S(2)}, u32[]{:S(2)}) %collective-permute-start.5) | collective-permute-done | bytes 294944 | tf_op jit(solution)/shard_map/ppermute | solution.py:92
  159.1 1.9 collective-permute-start.9
  161.0 12.9 %collective-permute-done.6 = bf16[384,384]{1,0:T(8,128)(2,1)} collective-permute-done((bf16[384,384]{1,0:T(8,128)(2,1)S(1)}, bf16[384,384]{1,0:T(8,128)(2,1)}, u32[]{:S(2)}, u32[]{:S(2)}) %collective-permute-start.6) | collective-permute-done | bytes 294944 | tf_op jit(solution)/shard_map/ppermute | solution.py:92
  174.0 2.4 convolution_convert_fusion.1
  176.4 2.9 collective-permute-start.10
  179.3 4.8 %collective-permute-done.7 = bf16[384,384]{1,0:T(8,128)(2,1)} collective-permute-done((bf16[384,384]{1,0:T(8,128)(2,1)}, bf16[384,384]{1,0:T(8,128)(2,1)}, u32[]{:S(2)}, u32[]{:S(2)}) %collective-permute-start.7) | collective-permute-done | bytes 294944 | tf_op jit(solution)/shard_map/ppermute | solution.py:92
  184.1 1.0 constant_dynamic-update-slice_fusion.15
  185.1 1.0 constant_dynamic-update-slice_fusion.14
  186.3 1.0 constant_dynamic-update-slice_fusion.10
  187.3 1.0 constant_dynamic-update-slice_fusion.9
  188.4 1.0 constant_dynamic-update-slice_fusion.7
  189.4 1.0 constant_dynamic-update-slice_fusion.6
  190.6 1.0 constant_dynamic-update-slice_fusion.2
  191.6 1.0 constant_dynamic-update-slice_fusion.1
  192.7 2.1 constant_dynamic-slice_fusion
  194.8 8.1 %reshape.19 = bf16[6,512,6,64]{3,2,1,0:T(8,128)(2,1)} reshape(bf16[3072,384]{1,0:T(8,128)(2,1)} %constant_dynamic-slice_fusion) | data formatting | bytes 4718592 | tf_op jit(solution)/shard_map/reshape | solution.py:102
  202.9 7.1 %copy.15 = bf16[6,512,6,64]{1,3,2,0:T(8,128)(2,1)} copy(bf16[6,512,6,64]{3,2,1,0:T(8,128)(2,1)} %reshape.19) | data formatting | bytes 4718592
  210.0 8.1 %reshape.20 = bf16[6,512,6,64]{3,2,1,0:T(8,128)(2,1)} reshape(bf16[3072,384]{1,0:T(8,128)(2,1)} %all-gather.8.cloned.1.call-done) | data formatting | bytes 4718592 | tf_op jit(solution)/shard_map/reshape | solution.py:103
  218.1 7.1 %copy.16 = bf16[6,512,6,64]{1,3,2,0:T(8,128)(2,1)} copy(bf16[6,512,6,64]{3,2,1,0:T(8,128)(2,1)} %reshape.20) | data formatting | bytes 4718592
  225.3 51.8 %while.15 = (s32[]{:T(128)}, f32[6,384]{1,0:T(8,128)S(1)}, f32[6,384]{1,0:T(8,128)S(1)}, f32[384,6,64]{0,2,1:T(8,128)S(1)}, bf16[6,512,6,64]{1,3,2,0:T(8,128)(2,...) while((s32[]{:T(128)}, f32[6,384]{1,0:T(8,128)S(1)}, ...), condition=%wide.region_7.8_spmd.clone, body=%wide.region_4.7_spmd.clone.sunk | while | flops 311883264 | bytes 35439748 | solution.py:124
  225.3 3.9 %bitcast_reduce_fusion.2 = (f32[6,384]{1,0:T(8,128)S(1)}, f32[6,512,384]{2,1,0:T(8,128)}) fusion(bf16[384,6,64]{0,2,1:T(8,128)(2,1)S(1)} %get-tuple-element.183, bf16[6,512,6,64]{1,3,2,0:T(8,128)(2,1)} %get-tuple-element.182, s32[]{:T(128)} %get-tuple-element.169), kind=kOutput, calls=%fused_computation.1.clone.1 | convolution fusion | flops 153351936 | bytes 5416448 | tf_op jit(solution)/shard_map/while/body/eval_jaxpr/qhd,khd->hqk/dot_general | solution.py:109
  229.2 3.6 %fusion.86 = f32[384,6,64]{0,2,1:T(8,128)S(1)} fusion(f32[6,512,384]{2,1,0:T(8,128)} %get-tuple-element.158, f32[6,384]{1,0:T(8,128)S(1)} %get-tuple-element.179, f32[384,6,64]{0,2,1:T(8,128)S(1)} %get-tuple-element.172, bf16[6,512,6,64]{1,3,2,0:T(8,128)(2,1)} %get-tuple-element.184, s32[]{:T(128)} %get-tuple-element.169, ...), kind=kOutput, calls=%fused_computation.9.clone.1 | convolution fusion | flops 154976256 | bytes 6310401 | tf_op jit(solution)/shard_map/while/body/eval_jaxpr/hqk,khd->qhd/dot_general | solution.py:115
  233.9 3.9 %bitcast_reduce_fusion.2 = (f32[6,384]{1,0:T(8,128)S(1)}, f32[6,512,384]{2,1,0:T(8,128)}) fusion(bf16[384,6,64]{0,2,1:T(8,128)(2,1)S(1)} %get-tuple-element.183, bf16[6,512,6,64]{1,3,2,0:T(8,128)(2,1)} %get-tuple-element.182, s32[]{:T(128)} %get-tuple-element.169), kind=kOutput, calls=%fused_computation.1.clone.1 | convolution fusion | flops 153351936 | bytes 5416448 | tf_op jit(solution)/shard_map/while/body/eval_jaxpr/qhd,khd->hqk/dot_general | solution.py:109
  237.9 3.6 %fusion.86 = f32[384,6,64]{0,2,1:T(8,128)S(1)} fusion(f32[6,512,384]{2,1,0:T(8,128)} %get-tuple-element.158, f32[6,384]{1,0:T(8,128)S(1)} %get-tuple-element.179, f32[384,6,64]{0,2,1:T(8,128)S(1)} %get-tuple-element.172, bf16[6,512,6,64]{1,3,2,0:T(8,128)(2,1)} %get-tuple-element.184, s32[]{:T(128)} %get-tuple-element.169, ...), kind=kOutput, calls=%fused_computation.9.clone.1 | convolution fusion | flops 154976256 | bytes 6310401 | tf_op jit(solution)/shard_map/while/body/eval_jaxpr/hqk,khd->qhd/dot_general | solution.py:115
  242.5 3.9 %bitcast_reduce_fusion.2 = (f32[6,384]{1,0:T(8,128)S(1)}, f32[6,512,384]{2,1,0:T(8,128)}) fusion(bf16[384,6,64]{0,2,1:T(8,128)(2,1)S(1)} %get-tuple-element.183, bf16[6,512,6,64]{1,3,2,0:T(8,128)(2,1)} %get-tuple-element.182, s32[]{:T(128)} %get-tuple-element.169), kind=kOutput, calls=%fused_computation.1.clone.1 | convolution fusion | flops 153351936 | bytes 5416448 | tf_op jit(solution)/shard_map/while/body/eval_jaxpr/qhd,khd->hqk/dot_general | solution.py:109
  246.5 3.6 %fusion.86 = f32[384,6,64]{0,2,1:T(8,128)S(1)} fusion(f32[6,512,384]{2,1,0:T(8,128)} %get-tuple-element.158, f32[6,384]{1,0:T(8,128)S(1)} %get-tuple-element.179, f32[384,6,64]{0,2,1:T(8,128)S(1)} %get-tuple-element.172, bf16[6,512,6,64]{1,3,2,0:T(8,128)(2,1)} %get-tuple-element.184, s32[]{:T(128)} %get-tuple-element.169, ...), kind=kOutput, calls=%fused_computation.9.clone.1 | convolution fusion | flops 154976256 | bytes 6310401 | tf_op jit(solution)/shard_map/while/body/eval_jaxpr/hqk,khd->qhd/dot_general | solution.py:115
  251.2 3.9 %bitcast_reduce_fusion.2 = (f32[6,384]{1,0:T(8,128)S(1)}, f32[6,512,384]{2,1,0:T(8,128)}) fusion(bf16[384,6,64]{0,2,1:T(8,128)(2,1)S(1)} %get-tuple-element.183, bf16[6,512,6,64]{1,3,2,0:T(8,128)(2,1)} %get-tuple-element.182, s32[]{:T(128)} %get-tuple-element.169), kind=kOutput, calls=%fused_computation.1.clone.1 | convolution fusion | flops 153351936 | bytes 5416448 | tf_op jit(solution)/shard_map/while/body/eval_jaxpr/qhd,khd->hqk/dot_general | solution.py:109
  255.2 3.6 %fusion.86 = f32[384,6,64]{0,2,1:T(8,128)S(1)} fusion(f32[6,512,384]{2,1,0:T(8,128)} %get-tuple-element.158, f32[6,384]{1,0:T(8,128)S(1)} %get-tuple-element.179, f32[384,6,64]{0,2,1:T(8,128)S(1)} %get-tuple-element.172, bf16[6,512,6,64]{1,3,2,0:T(8,128)(2,1)} %get-tuple-element.184, s32[]{:T(128)} %get-tuple-element.169, ...), kind=kOutput, calls=%fused_computation.9.clone.1 | convolution fusion | flops 154976256 | bytes 6310401 | tf_op jit(solution)/shard_map/while/body/eval_jaxpr/hqk,khd->qhd/dot_general | solution.py:115
  259.8 3.9 %bitcast_reduce_fusion.2 = (f32[6,384]{1,0:T(8,128)S(1)}, f32[6,512,384]{2,1,0:T(8,128)}) fusion(bf16[384,6,64]{0,2,1:T(8,128)(2,1)S(1)} %get-tuple-element.183, bf16[6,512,6,64]{1,3,2,0:T(8,128)(2,1)} %get-tuple-element.182, s32[]{:T(128)} %get-tuple-element.169), kind=kOutput, calls=%fused_computation.1.clone.1 | convolution fusion | flops 153351936 | bytes 5416448 | tf_op jit(solution)/shard_map/while/body/eval_jaxpr/qhd,khd->hqk/dot_general | solution.py:109
  263.8 3.6 %fusion.86 = f32[384,6,64]{0,2,1:T(8,128)S(1)} fusion(f32[6,512,384]{2,1,0:T(8,128)} %get-tuple-element.158, f32[6,384]{1,0:T(8,128)S(1)} %get-tuple-element.179, f32[384,6,64]{0,2,1:T(8,128)S(1)} %get-tuple-element.172, bf16[6,512,6,64]{1,3,2,0:T(8,128)(2,1)} %get-tuple-element.184, s32[]{:T(128)} %get-tuple-element.169, ...), kind=kOutput, calls=%fused_computation.9.clone.1 | convolution fusion | flops 154976256 | bytes 6310401 | tf_op jit(solution)/shard_map/while/body/eval_jaxpr/hqk,khd->qhd/dot_general | solution.py:115
  268.5 3.9 %bitcast_reduce_fusion.2 = (f32[6,384]{1,0:T(8,128)S(1)}, f32[6,512,384]{2,1,0:T(8,128)}) fusion(bf16[384,6,64]{0,2,1:T(8,128)(2,1)S(1)} %get-tuple-element.183, bf16[6,512,6,64]{1,3,2,0:T(8,128)(2,1)} %get-tuple-element.182, s32[]{:T(128)} %get-tuple-element.169), kind=kOutput, calls=%fused_computation.1.clone.1 | convolution fusion | flops 153351936 | bytes 5416448 | tf_op jit(solution)/shard_map/while/body/eval_jaxpr/qhd,khd->hqk/dot_general | solution.py:109
  272.4 3.6 %fusion.86 = f32[384,6,64]{0,2,1:T(8,128)S(1)} fusion(f32[6,512,384]{2,1,0:T(8,128)} %get-tuple-element.158, f32[6,384]{1,0:T(8,128)S(1)} %get-tuple-element.179, f32[384,6,64]{0,2,1:T(8,128)S(1)} %get-tuple-element.172, bf16[6,512,6,64]{1,3,2,0:T(8,128)(2,1)} %get-tuple-element.184, s32[]{:T(128)} %get-tuple-element.169, ...), kind=kOutput, calls=%fused_computation.9.clone.1 | convolution fusion | flops 154976256 | bytes 6310401 | tf_op jit(solution)/shard_map/while/body/eval_jaxpr/hqk,khd->qhd/dot_general | solution.py:115
  277.2 2.0 convolution_convert_fusion
  279.2 30.1 %reduce-scatter.2.cloned.1.call-done = bf16[384,384]{0,1:T(8,128)(2,1)} async-done(((bf16[384,1536]{0,1:T(8,128)(2,1)}), bf16[384,384]{0,1:T(8,128)(2,1)}) %reduce-scatter.2.cloned.1.call-update) | async-done | bytes 294928 | tf_op jit(solution)/shard_map/reduce_scatter | solution.py:132
  309.3 1.0 add_convert_fusion
  310.3 0.9 copy.18
  (90 shorter events, 9.9 us)
Async XLA Ops:
  6.5 270.6 %copy-start = (bf16[384,1536]{1,0:T(8,128)(2,1)S(1)}, bf16[384,1536]{1,0:T(8,128)(2,1)}, u32[]{:S(2)}) copy-start(bf16[384,1536]{1,0:T(8,128)(2,1)} %param.15) | copy-start | bytes 3538948
  6.5 12.0 %copy-start.2 = (bf16[768,768]{1,0:T(8,128)(2,1)S(1)}, bf16[768,768]{1,0:T(8,128)(2,1)}, u32[]{:S(2)}) copy-start(bf16[768,768]{1,0:T(8,128)(2,1)} %param.9) | copy-start | bytes 3538948
  6.5 76.6 %all-gather.4.cloned.1.call-start = ((), (), s32[]{:S(2)}) async-start(), calls=%async_computation.1 | async-start | bytes 1474560 | tf_op jit(solution)/shard_map/all_gather | solution.py:52
  7.4 14.6 %collective-permute-start = (bf16[2,768]{1,0:T(2,128)(2,1)S(1)}, bf16[2,768]{1,0:T(2,128)(2,1)S(1)}, u32[]{:S(2)}, u32[]{:S(2)}) collective-permute-start(bf16[2,768]{1,0:T(2,128)(2,1)S(1)} %get-tuple-element.103), channel_id=1, source_target_pairs={{0,4},{4,8},{8,12},{12,16},{16,20},{20,24},{24,28},{1,5},{5,9},{9,... | collective-permute-start | bytes 9224 | tf_op jit(solution)/shard_map/ppermute | solution.py:19
  9.8 12.3 %collective-permute-start.1 = (bf16[2,768]{1,0:T(2,128)(2,1)S(1)}, bf16[2,768]{1,0:T(2,128)(2,1)}, u32[]{:S(2)}, u32[]{:S(2)}) collective-permute-start(bf16[2,768]{1,0:T(2,128)(2,1)S(1)} %get-tuple-element.104), channel_id=1, source_target_pairs={{4,0},{8,4},{12,8},{16,12},{20,16},{24,20},{28,24},{5,1},{9,5},{13... | collective-permute-start | bytes 9224 | tf_op jit(solution)/shard_map/ppermute | solution.py:22
  23.0 10.0 %copy-start.3 = (f32[384,384]{0,1:T(8,128)S(1)}, f32[384,384]{0,1:T(8,128)}, u32[]{:S(2)}) copy-start(f32[384,384]{0,1:T(8,128)} %fusion.44) | copy-start | bytes 1769476
  31.4 3.5 %copy-start.4 = (bf16[384,768]{1,0:T(8,128)(2,1)S(1)}, bf16[384,768]{1,0:T(8,128)(2,1)}, u32[]{:S(2)}) copy-start(bf16[384,768]{1,0:T(8,128)(2,1)} %slice.67) | copy-start | bytes 1769476
  33.0 3.4 %copy-start.5 = (bf16[384,768]{1,0:T(8,128)(2,1)S(1)}, bf16[384,768]{1,0:T(8,128)(2,1)}, u32[]{:S(2)}) copy-start(bf16[384,768]{1,0:T(8,128)(2,1)} %slice.69) | copy-start | bytes 1769476
  51.8 84.7 %all-gather.6.cloned.1.call-start = ((), (), s32[]{:S(2)}) async-start(), calls=%async_computation.2 | async-start | bytes 1474560 | tf_op jit(solution)/shard_map/all_gather | solution.py:67
  83.1 6.6 %copy-start.8 = (bf16[384,1536]{0,1:T(8,128)(2,1)S(1)}, bf16[384,1536]{0,1:T(8,128)(2,1)}, u32[]{:S(2)}) copy-start(bf16[384,1536]{0,1:T(8,128)(2,1)} %all-gather.4.cloned.1.call-done) | copy-start | bytes 3538948
  83.1 6.6 %copy-start.9 = (bf16[3,384,1536]{2,1,0:T(8,128)(2,1)S(1)}, bf16[3,384,1536]{2,1,0:T(8,128)(2,1)}, u32[]{:S(2)}) copy-start(bf16[3,384,1536]{2,1,0:T(8,128)(2,1)} %param.11) | copy-start | bytes 10616836
  84.6 5.2 %collective-permute-start.2 = (bf16[4,1536]{0,1:T(8,128)(2,1)S(1)}, bf16[4,1536]{0,1:T(8,128)(2,1)S(1)}, u32[]{:S(2)}, u32[]{:S(2)}) collective-permute-start(bf16[4,1536]{0,1:T(8,128)(2,1)S(1)} %get-tuple-element.102), channel_id=1, source_target_pairs={{0,4},{4,8},{8,12},{12,16},{16,20},{20,24},{24,28},{1,5},{5,9},{9,... | collective-permute-start | bytes 36872 | tf_op jit(solution)/shard_map/ppermute | solution.py:19
  86.0 5.3 %collective-permute-start.3 = (bf16[4,1536]{0,1:T(8,128)(2,1)S(1)}, bf16[4,1536]{0,1:T(8,128)(2,1)S(1)}, u32[]{:S(2)}, u32[]{:S(2)}) collective-permute-start(bf16[4,1536]{0,1:T(8,128)(2,1)S(1)} %get-tuple-element.101), channel_id=1, source_target_pairs={{4,0},{8,4},{12,8},{16,12},{20,16},{24,20},{28,24},{5,1},{9,5},{13... | collective-permute-start | bytes 36872 | tf_op jit(solution)/shard_map/ppermute | solution.py:22
  102.9 107.1 %all-gather.8.cloned.1.call-start = ((), (), s32[]{:S(2)}) async-start(), calls=%async_computation.3 | async-start | bytes 2654208 | tf_op jit(solution)/shard_map/all_gather | solution.py:98
  139.6 169.7 %reduce-scatter.2.cloned.1.call-start = ((), (), s32[]{:S(2)}) async-start(), calls=%async_computation.4 | async-start | bytes 1474560 | tf_op jit(solution)/shard_map/reduce_scatter | solution.py:132
  142.1 7.1 %collective-permute-start.4 = (bf16[384,384]{1,0:T(8,128)(2,1)S(1)}, bf16[384,384]{1,0:T(8,128)(2,1)S(1)}, u32[]{:S(2)}, u32[]{:S(2)}) collective-permute-start(bf16[384,384]{1,0:T(8,128)(2,1)S(1)} %convolution_convert_fusion.3), channel_id=1, source_target_pairs={{0,4},{4,8},{8,12},{12,16},{16,20},{20,24},{24,28},{28,0},{1,5},{5... | collective-permute-start | bytes 884744 | tf_op jit(solution)/shard_map/ppermute | solution.py:92
  149.2 9.2 %collective-permute-start.5 = (bf16[384,384]{1,0:T(8,128)(2,1)S(1)}, bf16[384,384]{1,0:T(8,128)(2,1)S(1)}, u32[]{:S(2)}, u32[]{:S(2)}) collective-permute-start(bf16[384,384]{1,0:T(8,128)(2,1)S(1)} %collective-permute-done.4), channel_id=1, source_target_pairs={{0,4},{4,8},{8,12},{12,16},{16,20},{20,24},{24,28},{28,0},{1,5},{5... | collective-permute-start | bytes 884744 | tf_op jit(solution)/shard_map/ppermute | solution.py:92
  149.2 9.2 %collective-permute-start.8 = (bf16[384,384]{1,0:T(8,128)(2,1)S(1)}, bf16[384,384]{1,0:T(8,128)(2,1)}, u32[]{:S(2)}, u32[]{:S(2)}) collective-permute-start(bf16[384,384]{1,0:T(8,128)(2,1)S(1)} %convolution_convert_fusion.3), channel_id=1, source_target_pairs={{0,28},{4,0},{8,4},{12,8},{16,12},{20,16},{24,20},{28,24},{1,29},{... | collective-permute-start | bytes 884744 | tf_op jit(solution)/shard_map/ppermute | solution.py:95
  158.4 0.7 copy-start.6
  158.4 15.6 %collective-permute-start.6 = (bf16[384,384]{1,0:T(8,128)(2,1)S(1)}, bf16[384,384]{1,0:T(8,128)(2,1)}, u32[]{:S(2)}, u32[]{:S(2)}) collective-permute-start(bf16[384,384]{1,0:T(8,128)(2,1)S(1)} %collective-permute-done.5), channel_id=1, source_target_pairs={{0,4},{4,8},{8,12},{12,16},{16,20},{20,24},{24,28},{28,0},{1,5},{5... | collective-permute-start | bytes 884744 | tf_op jit(solution)/shard_map/ppermute | solution.py:92
  159.1 17.3 %collective-permute-start.9 = (bf16[384,384]{1,0:T(8,128)(2,1)}, bf16[384,384]{1,0:T(8,128)(2,1)}, u32[]{:S(2)}, u32[]{:S(2)}) collective-permute-start(bf16[384,384]{1,0:T(8,128)(2,1)} %collective-permute-done.8), channel_id=1, source_target_pairs={{0,28},{4,0},{8,4},{12,8},{16,12},{20,16},{24,20},{28,24},{1,29},{... | collective-permute-start | bytes 884744 | tf_op jit(solution)/shard_map/ppermute | solution.py:95
  174.0 10.2 %collective-permute-start.7 = (bf16[384,384]{1,0:T(8,128)(2,1)}, bf16[384,384]{1,0:T(8,128)(2,1)}, u32[]{:S(2)}, u32[]{:S(2)}) collective-permute-start(bf16[384,384]{1,0:T(8,128)(2,1)} %collective-permute-done.6), channel_id=1, source_target_pairs={{0,4},{4,8},{8,12},{12,16},{16,20},{20,24},{24,28},{28,0},{1,5},{5... | collective-permute-start | bytes 884744 | tf_op jit(solution)/shard_map/ppermute | solution.py:92
  174.0 12.2 %copy-start.7 = (bf16[384,384]{1,0:T(8,128)(2,1)S(1)}, bf16[384,384]{1,0:T(8,128)(2,1)}, u32[]{:S(2)}) copy-start(bf16[384,384]{1,0:T(8,128)(2,1)} %copy-done.6) | copy-start | bytes 884740
  176.4 11.9 %collective-permute-start.10 = (bf16[384,384]{1,0:T(8,128)(2,1)}, bf16[384,384]{1,0:T(8,128)(2,1)S(1)}, u32[]{:S(2)}, u32[]{:S(2)}) collective-permute-start(bf16[384,384]{1,0:T(8,128)(2,1)} %collective-permute-done.9), channel_id=1, source_target_pairs={{0,28},{4,0},{8,4},{12,8},{16,12},{20,16},{24,20},{28,24},{1,29},{... | collective-permute-start | bytes 884744 | tf_op jit(solution)/shard_map/ppermute | solution.py:95
  229.2 3.9 %copy-start.1 = (f32[6,512,384]{2,1,0:T(8,128)S(1)}, f32[6,512,384]{2,1,0:T(8,128)}, u32[]{:S(2)}) copy-start(f32[6,512,384]{2,1,0:T(8,128)} %get-tuple-element.158) | copy-start | bytes 14155780 | tf_op jit(solution)/shard_map/while
  237.9 3.9 %copy-start.1 = (f32[6,512,384]{2,1,0:T(8,128)S(1)}, f32[6,512,384]{2,1,0:T(8,128)}, u32[]{:S(2)}) copy-start(f32[6,512,384]{2,1,0:T(8,128)} %get-tuple-element.158) | copy-start | bytes 14155780 | tf_op jit(solution)/shard_map/while
  246.5 3.9 %copy-start.1 = (f32[6,512,384]{2,1,0:T(8,128)S(1)}, f32[6,512,384]{2,1,0:T(8,128)}, u32[]{:S(2)}) copy-start(f32[6,512,384]{2,1,0:T(8,128)} %get-tuple-element.158) | copy-start | bytes 14155780 | tf_op jit(solution)/shard_map/while
  255.1 3.9 %copy-start.1 = (f32[6,512,384]{2,1,0:T(8,128)S(1)}, f32[6,512,384]{2,1,0:T(8,128)}, u32[]{:S(2)}) copy-start(f32[6,512,384]{2,1,0:T(8,128)} %get-tuple-element.158) | copy-start | bytes 14155780 | tf_op jit(solution)/shard_map/while
  263.8 3.9 %copy-start.1 = (f32[6,512,384]{2,1,0:T(8,128)S(1)}, f32[6,512,384]{2,1,0:T(8,128)}, u32[]{:S(2)}) copy-start(f32[6,512,384]{2,1,0:T(8,128)} %get-tuple-element.158) | copy-start | bytes 14155780 | tf_op jit(solution)/shard_map/while
  272.4 3.9 %copy-start.1 = (f32[6,512,384]{2,1,0:T(8,128)S(1)}, f32[6,512,384]{2,1,0:T(8,128)}, u32[]{:S(2)}) copy-start(f32[6,512,384]{2,1,0:T(8,128)} %get-tuple-element.158) | copy-start | bytes 14155780 | tf_op jit(solution)/shard_map/while
Sparse Core Ops, SparseCore 0:
  51.9 31.1 all-gather.3
  103.0 33.3 all-gather.5
  139.7 35.6 all-gather.7
  279.3 29.9 reduce-scatter.1
